TPU v7x, 512 devices: a whole 4x4x16 slice. The times are simulated.
512 devices in a mesh: seq: 32 (over z, core), head: 16 (over y, x).
Axes of the slice: x: 4, y: 4, z: 16, core: 2. Of those that a mesh axis runs over, the one named last changes fastest.
Arguments:
- hidden_in: bfloat16 [8192, 4096], P('seq'), may hold values from -6 to 6
- w_qkv: bfloat16 [3, 4096, 4096], P(None, 'seq', 'head'), may hold values from -0.09375 to 0.09375
- doc_starts: int32 [9], replicated, may hold values from 0 to 8191, as said below
- beta_codes: int32 [8192, 32], P('seq', 'head'), may hold values from 0 to 4, as said below
- w_out: bfloat16 [4096, 4096], P('head', 'seq'), may hold values from -0.1875 to 0.1875
Outputs:
- layer_out: bfloat16 [8192, 4096], P('seq', 'head')
Inputs may be any that keep to these rules, and one draw needn't show every extreme that they name: `doc_starts`: strictly rising; the first is 0 and the last is 8191, a one-token final document. `beta_codes`: integer codes of the write strength beta = 1.6 + 0.1 * code.
All inputs are finite; a program needn't handle non-finite values.
Results may differ from a plain program's by a relative error of at most 0.02.
Values may be sent and summed in bfloat16 or wider, within the bound.
No kernel may reach another device: no remote copies, remote signals or barrier semaphores. Data moves between devices by JAX's collectives and lax.ppermute only.
A program may use at most 64 MiB of HBM per device.

v0:
```python
import jax
import jax.numpy as jnp
from jax import lax
from jax.sharding import PartitionSpec as P

highest_accuracy = lax.Precision.HIGHEST


def passed_along(value, axis, steps):
    count = lax.axis_size(axis)
    first, last = (max(0, -steps), min(count, count - steps))
    return lax.ppermute(value, axis, [(source, source + steps) for source in range(first, last)])


def bmatmul(left, right):
    return jnp.einsum("hij,hjk->hik", left, right, precision=highest_accuracy)


def unit_rows(matrix):
    return matrix * lax.rsqrt(jnp.sum(matrix * matrix, axis=-1, keepdims=True) + 1e-06)


def block_terms(query_blk, key_blk, value_blk, beta_blk, doc_blk):
    block_len = query_blk.shape[1]
    head_size = query_blk.shape[2]
    row_ids = lax.broadcasted_iota(jnp.int32, (block_len, block_len), 0)
    col_ids = lax.broadcasted_iota(jnp.int32, (block_len, block_len), 1)
    same_document = doc_blk[:, None] == doc_blk[None, :]
    strict_mask = same_document & (col_ids < row_ids)
    incl_mask = same_document & (col_ids <= row_ids)
    carry_in = (doc_blk == 0).astype(jnp.float32)
    last_doc = (doc_blk == doc_blk[-1]).astype(jnp.float32)
    last_keep = carry_in[-1]
    key_gram = jnp.einsum("hts,hus->htu", key_blk, key_blk, precision=highest_accuracy)
    system = jnp.eye(block_len, dtype=jnp.float32)[None] + jnp.where(
        strict_mask[None], beta_blk[:, :, None] * key_gram, 0.0
    )
    right_side = beta_blk[:, :, None] * jnp.concatenate(
        [value_blk, carry_in[None, :, None] * key_blk], axis=-1
    )
    solved = jax.scipy.linalg.solve_triangular(system, right_side, lower=True, unit_diagonal=True)
    fresh_vals = solved[..., :head_size]
    mixed_keys = solved[..., head_size:]
    query_key = jnp.where(
        incl_mask[None],
        jnp.einsum("hts,hus->htu", query_blk, key_blk, precision=highest_accuracy),
        0.0,
    )
    local_out = bmatmul(query_key, fresh_vals)
    carry_map = carry_in[None, :, None] * query_blk - bmatmul(query_key, mixed_keys)
    tail_keys = last_doc[None, :, None] * key_blk
    trans_map = last_keep * jnp.eye(head_size, dtype=jnp.float32)[None] - jnp.einsum(
        "hts,htu->hsu", tail_keys, mixed_keys, precision=highest_accuracy
    )
    state_add = jnp.einsum("hts,htv->hsv", tail_keys, fresh_vals, precision=highest_accuracy)
    return (carry_map, local_out, trans_map, state_add)


def per_device(hidden_in, w_qkv, doc_starts, beta_codes, w_out):
    tok_rows = hidden_in.shape[0]
    head_count = beta_codes.shape[1]
    feat_width = w_qkv.shape[2]
    head_size = feat_width // head_count
    projected = jnp.einsum(
        "td,pde->pte",
        hidden_in,
        lax.all_gather(w_qkv, "seq", axis=1, tiled=True),
        preferred_element_type=jnp.float32,
    ).astype(jnp.bfloat16)
    block_len = min(128, tok_rows)
    block_count = tok_rows // block_len

    def to_blocks(matrix):
        shaped = matrix.astype(jnp.float32).reshape(block_count, block_len, head_count, head_size)
        return jnp.transpose(shaped, (0, 2, 1, 3))

    queries = to_blocks(
        unit_rows(projected[0].astype(jnp.float32).reshape(tok_rows, head_count, head_size))
    )
    keys_all = to_blocks(
        unit_rows(projected[1].astype(jnp.float32).reshape(tok_rows, head_count, head_size))
    )
    values_all = to_blocks(projected[2])
    betas = 1.6 + 0.1 * beta_codes.astype(jnp.float32)
    betas = jnp.transpose(betas.reshape(block_count, block_len, head_count), (0, 2, 1))
    positions = lax.axis_index("seq") * tok_rows + jnp.arange(tok_rows, dtype=jnp.int32)
    is_start = jnp.any(positions[:, None] == doc_starts[None, :], axis=1).astype(jnp.int32)
    doc_index = jnp.cumsum(is_start.reshape(block_count, block_len), axis=1)
    blocks = (queries, keys_all, values_all, betas, doc_index)
    identity_mat = jnp.broadcast_to(
        jnp.eye(head_size, dtype=jnp.float32), (head_count, head_size, head_size)
    )
    zero_state = jnp.zeros((head_count, head_size, head_size), jnp.float32)

    def local_step(carry, block_in):
        transit, local_state = carry
        carry_map, local_out, trans_map, state_add = block_terms(*block_in)
        partial_out = local_out + bmatmul(carry_map, local_state)
        correction = bmatmul(carry_map, transit)
        return (
            (bmatmul(trans_map, transit), bmatmul(trans_map, local_state) + state_add),
            (partial_out, correction),
        )

    (transit, local_state), (partial_out, correction) = lax.scan(
        local_step, (identity_mat, zero_state), blocks
    )

    def relay(turn_index, incoming):
        return passed_along(
            (bmatmul(transit, incoming) + local_state).astype(jnp.bfloat16), "seq", 1
        ).astype(jnp.float32)

    state_in = lax.fori_loop(0, lax.axis_size("seq") - 1, relay, zero_state)

    def rerun_step(state_now, block_in):
        carry_map, local_out, trans_map, state_add = block_terms(*block_in)
        result = local_out + bmatmul(carry_map, state_now)
        return (bmatmul(trans_map, state_now) + state_add, result)

    final_state, outputs = lax.scan(rerun_step, state_in, blocks)
    outputs = jnp.transpose(outputs, (0, 2, 1, 3)).reshape(tok_rows, head_count, head_size)
    normed = outputs * lax.rsqrt(jnp.mean(outputs * outputs, axis=-1, keepdims=True) + 1e-05)
    normed = normed.astype(jnp.bfloat16).reshape(tok_rows, feat_width)
    terms = jnp.dot(
        normed, lax.all_gather(w_out, "seq", axis=1, tiled=True), preferred_element_type=jnp.float32
    )
    return lax.psum_scatter(terms.astype(jnp.bfloat16), "head", scatter_dimension=1, tiled=True)


def solution(mesh):
    in_specs = (P("seq", None), P(None, "seq", "head"), P(), P("seq", "head"), P("head", "seq"))
    out_specs = P("seq", "head")
    return jax.shard_map(
        per_device, mesh=mesh, in_specs=in_specs, out_specs=out_specs, check_vma=False
    )
```

profile of v0, /device:TPU:2, one launch (start us, length us, event | category | flops | bytes accessed | tf_op | source)
XLA Modules:
  0.0 534.2 jit_solution(8153678685199269172)
XLA Ops:
  11.1 91.4 %all-gather.3.cloned.1.call-done = bf16[3,4096,256]{1,2,0:T(8,128)(2,1)} async-done(((bf16[3,128,256]{1,2,0:T(8,128)(2,1)}), bf16[3,4096,256]{1,2,0:T(8,128)(2,1)}) %all-gather.3.cloned.1.call-update) | async-done | bytes 6291472 | tf_op jit(solution)/shard_map/all_gather | solution.py:67
  114.2 49.7 %while.37 = (s32[]{:T(128)}, f32[2,128,128]{2,1,0:T(8,128)S(1)}, f32[2,128,128]{2,1,0:T(8,128)S(1)}, s32[2,128]{1,0:T(2,128)S(1)}, f32[2,2,128,128]{3,2,1,0:T(8,...) while((s32[]{:T(128)}, f32[2,128,128]{2,1,0:T(8,128)S(1)}, ...), condition=%wide.region_4.6_spmd.clone, body=%wide.region_3.5_spmd.clone.sunk | while | flops 352977536 | bytes 3876507 | solution.py:105
  115.0 19.7 %custom-call.12 = f32[2,1,128,128]{2,3,1,0:T(8,128)S(1)} custom-call(f32[2,1,128,128]{3,2,1,0:T(8,128)S(1)} %fusion.169), custom_call_target="InvertDiagBlocksLowerTriangular" | custom-call | tf_op jit(solution)/shard_map/while/body/eval_jaxpr/jit(_solve_triangular)/vmap()/triangular_solve | solution.py:41
  139.7 19.7 %custom-call.12 = f32[2,1,128,128]{2,3,1,0:T(8,128)S(1)} custom-call(f32[2,1,128,128]{3,2,1,0:T(8,128)S(1)} %fusion.169), custom_call_target="InvertDiagBlocksLowerTriangular" | custom-call | tf_op jit(solution)/shard_map/while/body/eval_jaxpr/jit(_solve_triangular)/vmap()/triangular_solve | solution.py:41
  163.8 194.0 %while.38 = (s32[]{:T(128)}, f32[2,128,128]{2,1,0:T(8,128)S(1)}, f32[2,128,128]{2,1,0:T(8,128)S(1)}, f32[2,128,128]{2,1,0:T(8,128)S(1)}, s32[]{:T(128)}, /*index=5*/s32[]{:T(128)}) while((s32[]{:T(128)}, f32[2,128,128]{2,1,0:T(8,128)S(1)}, f32[2,128,128]{2,1,0:T(8,128)S(1)}, f32[2,128,128]{2,1,0:T(8,128)S(1)}, s32[]{:T(128)}, ...), condition=%wide.region_6.8_spmd.clone, body=%wide.region_5.7_spmd.clone.sunk | while | flops 50462720 | bytes 917623 | solution.py:114
  200.8 4.7 collective-permute-start
  259.7 4.8 collective-permute-start
  265.7 5.9 %collective-permute-start = (bf16[2,128,128]{2,1,0:T(8,128)(2,1)S(1)}, bf16[2,128,128]{2,1,0:T(8,128)(2,1)S(1)}, u32[]{:S(2)}, u32[]{:S(2)}) collective-permute-start(bf16[2,128,128]{2,1,0:T(8,128)(2,1)S(1)} %fusion.176), channel_id=1, source_target_pairs={{0,16},{16,32},{32,48},{48,64},{64,80},{80,96},{96,112},{112,128},... | collective-permute-start | bytes 196616 | tf_op jit(solution)/shard_map/while/body/eval_jaxpr/ppermute | solution.py:12
  272.8 5.9 %collective-permute-start = (bf16[2,128,128]{2,1,0:T(8,128)(2,1)S(1)}, bf16[2,128,128]{2,1,0:T(8,128)(2,1)S(1)}, u32[]{:S(2)}, u32[]{:S(2)}) collective-permute-start(bf16[2,128,128]{2,1,0:T(8,128)(2,1)S(1)} %fusion.176), channel_id=1, source_target_pairs={{0,16},{16,32},{32,48},{48,64},{64,80},{80,96},{96,112},{112,128},... | collective-permute-start | bytes 196616 | tf_op jit(solution)/shard_map/while/body/eval_jaxpr/ppermute | solution.py:12
  279.9 5.9 %collective-permute-start = (bf16[2,128,128]{2,1,0:T(8,128)(2,1)S(1)}, bf16[2,128,128]{2,1,0:T(8,128)(2,1)S(1)}, u32[]{:S(2)}, u32[]{:S(2)}) collective-permute-start(bf16[2,128,128]{2,1,0:T(8,128)(2,1)S(1)} %fusion.176), channel_id=1, source_target_pairs={{0,16},{16,32},{32,48},{48,64},{64,80},{80,96},{96,112},{112,128},... | collective-permute-start | bytes 196616 | tf_op jit(solution)/shard_map/while/body/eval_jaxpr/ppermute | solution.py:12
  287.0 5.9 %collective-permute-start = (bf16[2,128,128]{2,1,0:T(8,128)(2,1)S(1)}, bf16[2,128,128]{2,1,0:T(8,128)(2,1)S(1)}, u32[]{:S(2)}, u32[]{:S(2)}) collective-permute-start(bf16[2,128,128]{2,1,0:T(8,128)(2,1)S(1)} %fusion.176), channel_id=1, source_target_pairs={{0,16},{16,32},{32,48},{48,64},{64,80},{80,96},{96,112},{112,128},... | collective-permute-start | bytes 196616 | tf_op jit(solution)/shard_map/while/body/eval_jaxpr/ppermute | solution.py:12
  294.2 5.9 %collective-permute-start = (bf16[2,128,128]{2,1,0:T(8,128)(2,1)S(1)}, bf16[2,128,128]{2,1,0:T(8,128)(2,1)S(1)}, u32[]{:S(2)}, u32[]{:S(2)}) collective-permute-start(bf16[2,128,128]{2,1,0:T(8,128)(2,1)S(1)} %fusion.176), channel_id=1, source_target_pairs={{0,16},{16,32},{32,48},{48,64},{64,80},{80,96},{96,112},{112,128},... | collective-permute-start | bytes 196616 | tf_op jit(solution)/shard_map/while/body/eval_jaxpr/ppermute | solution.py:12
  301.3 5.9 %collective-permute-start = (bf16[2,128,128]{2,1,0:T(8,128)(2,1)S(1)}, bf16[2,128,128]{2,1,0:T(8,128)(2,1)S(1)}, u32[]{:S(2)}, u32[]{:S(2)}) collective-permute-start(bf16[2,128,128]{2,1,0:T(8,128)(2,1)S(1)} %fusion.176), channel_id=1, source_target_pairs={{0,16},{16,32},{32,48},{48,64},{64,80},{80,96},{96,112},{112,128},... | collective-permute-start | bytes 196616 | tf_op jit(solution)/shard_map/while/body/eval_jaxpr/ppermute | solution.py:12
  308.4 5.9 %collective-permute-start = (bf16[2,128,128]{2,1,0:T(8,128)(2,1)S(1)}, bf16[2,128,128]{2,1,0:T(8,128)(2,1)S(1)}, u32[]{:S(2)}, u32[]{:S(2)}) collective-permute-start(bf16[2,128,128]{2,1,0:T(8,128)(2,1)S(1)} %fusion.176), channel_id=1, source_target_pairs={{0,16},{16,32},{32,48},{48,64},{64,80},{80,96},{96,112},{112,128},... | collective-permute-start | bytes 196616 | tf_op jit(solution)/shard_map/while/body/eval_jaxpr/ppermute | solution.py:12
  315.5 5.9 %collective-permute-start = (bf16[2,128,128]{2,1,0:T(8,128)(2,1)S(1)}, bf16[2,128,128]{2,1,0:T(8,128)(2,1)S(1)}, u32[]{:S(2)}, u32[]{:S(2)}) collective-permute-start(bf16[2,128,128]{2,1,0:T(8,128)(2,1)S(1)} %fusion.176), channel_id=1, source_target_pairs={{0,16},{16,32},{32,48},{48,64},{64,80},{80,96},{96,112},{112,128},... | collective-permute-start | bytes 196616 | tf_op jit(solution)/shard_map/while/body/eval_jaxpr/ppermute | solution.py:12
  322.6 5.9 %collective-permute-start = (bf16[2,128,128]{2,1,0:T(8,128)(2,1)S(1)}, bf16[2,128,128]{2,1,0:T(8,128)(2,1)S(1)}, u32[]{:S(2)}, u32[]{:S(2)}) collective-permute-start(bf16[2,128,128]{2,1,0:T(8,128)(2,1)S(1)} %fusion.176), channel_id=1, source_target_pairs={{0,16},{16,32},{32,48},{48,64},{64,80},{80,96},{96,112},{112,128},... | collective-permute-start | bytes 196616 | tf_op jit(solution)/shard_map/while/body/eval_jaxpr/ppermute | solution.py:12
  329.7 5.9 %collective-permute-start = (bf16[2,128,128]{2,1,0:T(8,128)(2,1)S(1)}, bf16[2,128,128]{2,1,0:T(8,128)(2,1)S(1)}, u32[]{:S(2)}, u32[]{:S(2)}) collective-permute-start(bf16[2,128,128]{2,1,0:T(8,128)(2,1)S(1)} %fusion.176), channel_id=1, source_target_pairs={{0,16},{16,32},{32,48},{48,64},{64,80},{80,96},{96,112},{112,128},... | collective-permute-start | bytes 196616 | tf_op jit(solution)/shard_map/while/body/eval_jaxpr/ppermute | solution.py:12
  336.8 5.9 %collective-permute-start = (bf16[2,128,128]{2,1,0:T(8,128)(2,1)S(1)}, bf16[2,128,128]{2,1,0:T(8,128)(2,1)S(1)}, u32[]{:S(2)}, u32[]{:S(2)}) collective-permute-start(bf16[2,128,128]{2,1,0:T(8,128)(2,1)S(1)} %fusion.176), channel_id=1, source_target_pairs={{0,16},{16,32},{32,48},{48,64},{64,80},{80,96},{96,112},{112,128},... | collective-permute-start | bytes 196616 | tf_op jit(solution)/shard_map/while/body/eval_jaxpr/ppermute | solution.py:12
  343.9 5.9 %collective-permute-start = (bf16[2,128,128]{2,1,0:T(8,128)(2,1)S(1)}, bf16[2,128,128]{2,1,0:T(8,128)(2,1)S(1)}, u32[]{:S(2)}, u32[]{:S(2)}) collective-permute-start(bf16[2,128,128]{2,1,0:T(8,128)(2,1)S(1)} %fusion.176), channel_id=1, source_target_pairs={{0,16},{16,32},{32,48},{48,64},{64,80},{80,96},{96,112},{112,128},... | collective-permute-start | bytes 196616 | tf_op jit(solution)/shard_map/while/body/eval_jaxpr/ppermute | solution.py:12
  351.0 5.9 %collective-permute-start = (bf16[2,128,128]{2,1,0:T(8,128)(2,1)S(1)}, bf16[2,128,128]{2,1,0:T(8,128)(2,1)S(1)}, u32[]{:S(2)}, u32[]{:S(2)}) collective-permute-start(bf16[2,128,128]{2,1,0:T(8,128)(2,1)S(1)} %fusion.176), channel_id=1, source_target_pairs={{0,16},{16,32},{32,48},{48,64},{64,80},{80,96},{96,112},{112,128},... | collective-permute-start | bytes 196616 | tf_op jit(solution)/shard_map/while/body/eval_jaxpr/ppermute | solution.py:12
  357.8 52.2 %while.36 = (s32[]{:T(128)}, f32[2,128,128]{2,1,0:T(8,128)S(1)}, f32[2,2,128,128]{3,2,1,0:T(8,128)}, s32[2,128]{1,0:T(2,128)S(1)}, f32[2,2,128,128]{3,2,1,0:T(8,...) while((s32[]{:T(128)}, f32[2,128,128]{2,1,0:T(8,128)S(1)}, ...), condition=%wide.region_9.11_spmd, body=%wide.region_8.10_spmd.sunk | while | flops 504103552 | bytes 7187665 | solution.py:121
  358.4 19.7 %custom-call.11 = f32[2,1,128,128]{2,3,1,0:T(8,128)S(1)} custom-call(f32[2,1,128,128]{3,2,1,0:T(8,128)S(1)} %fusion.154), custom_call_target="InvertDiagBlocksLowerTriangular" | custom-call | tf_op jit(solution)/shard_map/while/body/eval_jaxpr/jit(_solve_triangular)/vmap()/triangular_solve | solution.py:41
  384.5 19.7 %custom-call.11 = f32[2,1,128,128]{2,3,1,0:T(8,128)S(1)} custom-call(f32[2,1,128,128]{3,2,1,0:T(8,128)S(1)} %fusion.154), custom_call_target="InvertDiagBlocksLowerTriangular" | custom-call | tf_op jit(solution)/shard_map/while/body/eval_jaxpr/jit(_solve_triangular)/vmap()/triangular_solve | solution.py:41
  416.5 111.2 %reduce-scatter.2.cloned.1.call-done = bf16[256,256]{1,0:T(8,128)(2,1)} async-done(((bf16[256,4096]{1,0:T(8,128)(2,1)}), bf16[256,256]{1,0:T(8,128)(2,1)}) %reduce-scatter.2.cloned.1.call-update) | async-done | bytes 131088 | tf_op jit(solution)/shard_map/reduce_scatter | solution.py:128
  (235 shorter events, 151.4 us)
Async XLA Ops:
  6.5 95.9 %all-gather.3.cloned.1.call-start = ((), (), s32[]{:S(2)}) async-start(), calls=%async_computation.1 | async-start | bytes 6488064 | tf_op jit(solution)/shard_map/all_gather | solution.py:67
  8.5 404.0 %all-gather.5.cloned.1.call-start = ((), (), s32[]{:S(2)}) async-start(), calls=%async_computation.2 | async-start | bytes 2162688 | tf_op jit(solution)/shard_map/all_gather | solution.py:126
  9.2 518.5 %reduce-scatter.2.cloned.1.call-start = ((), (), s32[]{:S(2)}) async-start(), calls=%async_computation.3 | async-start | bytes 2228224 | tf_op jit(solution)/shard_map/reduce_scatter | solution.py:128
  177.2 5.6 %collective-permute-start = (bf16[2,128,128]{2,1,0:T(8,128)(2,1)S(1)}, bf16[2,128,128]{2,1,0:T(8,128)(2,1)S(1)}, u32[]{:S(2)}, u32[]{:S(2)}) collective-permute-start(bf16[2,128,128]{2,1,0:T(8,128)(2,1)S(1)} %fusion.176), channel_id=1, source_target_pairs={{0,16},{16,32},{32,48},{48,64},{64,80},{80,96},{96,112},{112,128},... | collective-permute-start | bytes 196616 | tf_op jit(solution)/shard_map/while/body/eval_jaxpr/ppermute | solution.py:12
  200.8 5.6 %collective-permute-start = (bf16[2,128,128]{2,1,0:T(8,128)(2,1)S(1)}, bf16[2,128,128]{2,1,0:T(8,128)(2,1)S(1)}, u32[]{:S(2)}, u32[]{:S(2)}) collective-permute-start(bf16[2,128,128]{2,1,0:T(8,128)(2,1)S(1)} %fusion.176), channel_id=1, source_target_pairs={{0,16},{16,32},{32,48},{48,64},{64,80},{80,96},{96,112},{112,128},... | collective-permute-start | bytes 196616 | tf_op jit(solution)/shard_map/while/body/eval_jaxpr/ppermute | solution.py:12
  206.7 5.6 %collective-permute-start = (bf16[2,128,128]{2,1,0:T(8,128)(2,1)S(1)}, bf16[2,128,128]{2,1,0:T(8,128)(2,1)S(1)}, u32[]{:S(2)}, u32[]{:S(2)}) collective-permute-start(bf16[2,128,128]{2,1,0:T(8,128)(2,1)S(1)} %fusion.176), channel_id=1, source_target_pairs={{0,16},{16,32},{32,48},{48,64},{64,80},{80,96},{96,112},{112,128},... | collective-permute-start | bytes 196616 | tf_op jit(solution)/shard_map/while/body/eval_jaxpr/ppermute | solution.py:12
  212.6 5.6 %collective-permute-start = (bf16[2,128,128]{2,1,0:T(8,128)(2,1)S(1)}, bf16[2,128,128]{2,1,0:T(8,128)(2,1)S(1)}, u32[]{:S(2)}, u32[]{:S(2)}) collective-permute-start(bf16[2,128,128]{2,1,0:T(8,128)(2,1)S(1)} %fusion.176), channel_id=1, source_target_pairs={{0,16},{16,32},{32,48},{48,64},{64,80},{80,96},{96,112},{112,128},... | collective-permute-start | bytes 196616 | tf_op jit(solution)/shard_map/while/body/eval_jaxpr/ppermute | solution.py:12
  242.0 5.6 %collective-permute-start = (bf16[2,128,128]{2,1,0:T(8,128)(2,1)S(1)}, bf16[2,128,128]{2,1,0:T(8,128)(2,1)S(1)}, u32[]{:S(2)}, u32[]{:S(2)}) collective-permute-start(bf16[2,128,128]{2,1,0:T(8,128)(2,1)S(1)} %fusion.176), channel_id=1, source_target_pairs={{0,16},{16,32},{32,48},{48,64},{64,80},{80,96},{96,112},{112,128},... | collective-permute-start | bytes 196616 | tf_op jit(solution)/shard_map/while/body/eval_jaxpr/ppermute | solution.py:12
  247.9 5.6 %collective-permute-start = (bf16[2,128,128]{2,1,0:T(8,128)(2,1)S(1)}, bf16[2,128,128]{2,1,0:T(8,128)(2,1)S(1)}, u32[]{:S(2)}, u32[]{:S(2)}) collective-permute-start(bf16[2,128,128]{2,1,0:T(8,128)(2,1)S(1)} %fusion.176), channel_id=1, source_target_pairs={{0,16},{16,32},{32,48},{48,64},{64,80},{80,96},{96,112},{112,128},... | collective-permute-start | bytes 196616 | tf_op jit(solution)/shard_map/while/body/eval_jaxpr/ppermute | solution.py:12
  253.8 5.6 %collective-permute-start = (bf16[2,128,128]{2,1,0:T(8,128)(2,1)S(1)}, bf16[2,128,128]{2,1,0:T(8,128)(2,1)S(1)}, u32[]{:S(2)}, u32[]{:S(2)}) collective-permute-start(bf16[2,128,128]{2,1,0:T(8,128)(2,1)S(1)} %fusion.176), channel_id=1, source_target_pairs={{0,16},{16,32},{32,48},{48,64},{64,80},{80,96},{96,112},{112,128},... | collective-permute-start | bytes 196616 | tf_op jit(solution)/shard_map/while/body/eval_jaxpr/ppermute | solution.py:12
  259.7 5.7 %collective-permute-start = (bf16[2,128,128]{2,1,0:T(8,128)(2,1)S(1)}, bf16[2,128,128]{2,1,0:T(8,128)(2,1)S(1)}, u32[]{:S(2)}, u32[]{:S(2)}) collective-permute-start(bf16[2,128,128]{2,1,0:T(8,128)(2,1)S(1)} %fusion.176), channel_id=1, source_target_pairs={{0,16},{16,32},{32,48},{48,64},{64,80},{80,96},{96,112},{112,128},... | collective-permute-start | bytes 196616 | tf_op jit(solution)/shard_map/while/body/eval_jaxpr/ppermute | solution.py:12
  265.7 6.8 %collective-permute-start = (bf16[2,128,128]{2,1,0:T(8,128)(2,1)S(1)}, bf16[2,128,128]{2,1,0:T(8,128)(2,1)S(1)}, u32[]{:S(2)}, u32[]{:S(2)}) collective-permute-start(bf16[2,128,128]{2,1,0:T(8,128)(2,1)S(1)} %fusion.176), channel_id=1, source_target_pairs={{0,16},{16,32},{32,48},{48,64},{64,80},{80,96},{96,112},{112,128},... | collective-permute-start | bytes 196616 | tf_op jit(solution)/shard_map/while/body/eval_jaxpr/ppermute | solution.py:12
  272.8 6.8 %collective-permute-start = (bf16[2,128,128]{2,1,0:T(8,128)(2,1)S(1)}, bf16[2,128,128]{2,1,0:T(8,128)(2,1)S(1)}, u32[]{:S(2)}, u32[]{:S(2)}) collective-permute-start(bf16[2,128,128]{2,1,0:T(8,128)(2,1)S(1)} %fusion.176), channel_id=1, source_target_pairs={{0,16},{16,32},{32,48},{48,64},{64,80},{80,96},{96,112},{112,128},... | collective-permute-start | bytes 196616 | tf_op jit(solution)/shard_map/while/body/eval_jaxpr/ppermute | solution.py:12
  279.9 6.8 %collective-permute-start = (bf16[2,128,128]{2,1,0:T(8,128)(2,1)S(1)}, bf16[2,128,128]{2,1,0:T(8,128)(2,1)S(1)}, u32[]{:S(2)}, u32[]{:S(2)}) collective-permute-start(bf16[2,128,128]{2,1,0:T(8,128)(2,1)S(1)} %fusion.176), channel_id=1, source_target_pairs={{0,16},{16,32},{32,48},{48,64},{64,80},{80,96},{96,112},{112,128},... | collective-permute-start | bytes 196616 | tf_op jit(solution)/shard_map/while/body/eval_jaxpr/ppermute | solution.py:12
  287.0 6.8 %collective-permute-start = (bf16[2,128,128]{2,1,0:T(8,128)(2,1)S(1)}, bf16[2,128,128]{2,1,0:T(8,128)(2,1)S(1)}, u32[]{:S(2)}, u32[]{:S(2)}) collective-permute-start(bf16[2,128,128]{2,1,0:T(8,128)(2,1)S(1)} %fusion.176), channel_id=1, source_target_pairs={{0,16},{16,32},{32,48},{48,64},{64,80},{80,96},{96,112},{112,128},... | collective-permute-start | bytes 196616 | tf_op jit(solution)/shard_map/while/body/eval_jaxpr/ppermute | solution.py:12
  294.2 6.8 %collective-permute-start = (bf16[2,128,128]{2,1,0:T(8,128)(2,1)S(1)}, bf16[2,128,128]{2,1,0:T(8,128)(2,1)S(1)}, u32[]{:S(2)}, u32[]{:S(2)}) collective-permute-start(bf16[2,128,128]{2,1,0:T(8,128)(2,1)S(1)} %fusion.176), channel_id=1, source_target_pairs={{0,16},{16,32},{32,48},{48,64},{64,80},{80,96},{96,112},{112,128},... | collective-permute-start | bytes 196616 | tf_op jit(solution)/shard_map/while/body/eval_jaxpr/ppermute | solution.py:12
  301.3 6.8 %collective-permute-start = (bf16[2,128,128]{2,1,0:T(8,128)(2,1)S(1)}, bf16[2,128,128]{2,1,0:T(8,128)(2,1)S(1)}, u32[]{:S(2)}, u32[]{:S(2)}) collective-permute-start(bf16[2,128,128]{2,1,0:T(8,128)(2,1)S(1)} %fusion.176), channel_id=1, source_target_pairs={{0,16},{16,32},{32,48},{48,64},{64,80},{80,96},{96,112},{112,128},... | collective-permute-start | bytes 196616 | tf_op jit(solution)/shard_map/while/body/eval_jaxpr/ppermute | solution.py:12
  308.4 6.8 %collective-permute-start = (bf16[2,128,128]{2,1,0:T(8,128)(2,1)S(1)}, bf16[2,128,128]{2,1,0:T(8,128)(2,1)S(1)}, u32[]{:S(2)}, u32[]{:S(2)}) collective-permute-start(bf16[2,128,128]{2,1,0:T(8,128)(2,1)S(1)} %fusion.176), channel_id=1, source_target_pairs={{0,16},{16,32},{32,48},{48,64},{64,80},{80,96},{96,112},{112,128},... | collective-permute-start | bytes 196616 | tf_op jit(solution)/shard_map/while/body/eval_jaxpr/ppermute | solution.py:12
  315.5 6.8 %collective-permute-start = (bf16[2,128,128]{2,1,0:T(8,128)(2,1)S(1)}, bf16[2,128,128]{2,1,0:T(8,128)(2,1)S(1)}, u32[]{:S(2)}, u32[]{:S(2)}) collective-permute-start(bf16[2,128,128]{2,1,0:T(8,128)(2,1)S(1)} %fusion.176), channel_id=1, source_target_pairs={{0,16},{16,32},{32,48},{48,64},{64,80},{80,96},{96,112},{112,128},... | collective-permute-start | bytes 196616 | tf_op jit(solution)/shard_map/while/body/eval_jaxpr/ppermute | solution.py:12
  322.6 6.8 %collective-permute-start = (bf16[2,128,128]{2,1,0:T(8,128)(2,1)S(1)}, bf16[2,128,128]{2,1,0:T(8,128)(2,1)S(1)}, u32[]{:S(2)}, u32[]{:S(2)}) collective-permute-start(bf16[2,128,128]{2,1,0:T(8,128)(2,1)S(1)} %fusion.176), channel_id=1, source_target_pairs={{0,16},{16,32},{32,48},{48,64},{64,80},{80,96},{96,112},{112,128},... | collective-permute-start | bytes 196616 | tf_op jit(solution)/shard_map/while/body/eval_jaxpr/ppermute | solution.py:12
  329.7 6.8 %collective-permute-start = (bf16[2,128,128]{2,1,0:T(8,128)(2,1)S(1)}, bf16[2,128,128]{2,1,0:T(8,128)(2,1)S(1)}, u32[]{:S(2)}, u32[]{:S(2)}) collective-permute-start(bf16[2,128,128]{2,1,0:T(8,128)(2,1)S(1)} %fusion.176), channel_id=1, source_target_pairs={{0,16},{16,32},{32,48},{48,64},{64,80},{80,96},{96,112},{112,128},... | collective-permute-start | bytes 196616 | tf_op jit(solution)/shard_map/while/body/eval_jaxpr/ppermute | solution.py:12
  336.8 6.8 %collective-permute-start = (bf16[2,128,128]{2,1,0:T(8,128)(2,1)S(1)}, bf16[2,128,128]{2,1,0:T(8,128)(2,1)S(1)}, u32[]{:S(2)}, u32[]{:S(2)}) collective-permute-start(bf16[2,128,128]{2,1,0:T(8,128)(2,1)S(1)} %fusion.176), channel_id=1, source_target_pairs={{0,16},{16,32},{32,48},{48,64},{64,80},{80,96},{96,112},{112,128},... | collective-permute-start | bytes 196616 | tf_op jit(solution)/shard_map/while/body/eval_jaxpr/ppermute | solution.py:12
  343.9 6.8 %collective-permute-start = (bf16[2,128,128]{2,1,0:T(8,128)(2,1)S(1)}, bf16[2,128,128]{2,1,0:T(8,128)(2,1)S(1)}, u32[]{:S(2)}, u32[]{:S(2)}) collective-permute-start(bf16[2,128,128]{2,1,0:T(8,128)(2,1)S(1)} %fusion.176), channel_id=1, source_target_pairs={{0,16},{16,32},{32,48},{48,64},{64,80},{80,96},{96,112},{112,128},... | collective-permute-start | bytes 196616 | tf_op jit(solution)/shard_map/while/body/eval_jaxpr/ppermute | solution.py:12
  351.0 6.8 %collective-permute-start = (bf16[2,128,128]{2,1,0:T(8,128)(2,1)S(1)}, bf16[2,128,128]{2,1,0:T(8,128)(2,1)S(1)}, u32[]{:S(2)}, u32[]{:S(2)}) collective-permute-start(bf16[2,128,128]{2,1,0:T(8,128)(2,1)S(1)} %fusion.176), channel_id=1, source_target_pairs={{0,16},{16,32},{32,48},{48,64},{64,80},{80,96},{96,112},{112,128},... | collective-permute-start | bytes 196616 | tf_op jit(solution)/shard_map/while/body/eval_jaxpr/ppermute | solution.py:12
  (16 other events, 352.2 us)
Sparse Core Ops, SparseCore 0:
  9.4 92.9 all-gather.2
  104.5 69.6 all-gather.4
  416.6 111.0 reduce-scatter.1
where the time goes:
time: 535 us; the launch traced here: 534 us
  waiting for transfers between devices  231 us (43%)
  starting transfers between devices  157 us (29%)
  other arithmetic  90.8 us (17%)
  matrix products  27.9 us (5%)
  between operations  13.3 us (2%)
  local copies, waits for them, and re-layouts  12.8 us (2%)
    ppermute x31, starting transfers between devices, passed_along(): lax.ppermute(value, axis, [(source, source + steps) for source in range(f...  157 us
    reduce_scatter x1, waiting for transfers between devices, per_device(): lax.psum_scatter(terms.astype(jnp.bfloat16), 'head', scatter_dimension=1,...  111 us
    all_gather x1, waiting for transfers between devices, per_device(): lax.all_gather(w_qkv, 'seq', axis=1, tiled=True)  91.4 us
    another operation x10, other arithmetic, block_terms(): jax.scipy.linalg.solve_triangular(system, right_side, lower=True, unit_di...  78.9 us
    ppermute x31, waiting for transfers between devices, passed_along(): lax.ppermute(value, axis, [(source, source + steps) for source in range(f...  27.3 us
    dot_general x43, matrix products, bmatmul(): return jnp.einsum('hij,hjk->hik', left, right, precision=highest_accuracy)  11.6 us
  transfers between devices with their start and end apart: 34, of which 33 were waited for; matrix products, arithmetic and copies ran while one was open for 24% of the time, Pallas kernels for 0%

commit v1 on v0

--- a/solution.py
+++ b/solution.py
@@ -64,7 +64,9 @@
     projected = jnp.einsum(
         "td,pde->pte",
         hidden_in,
-        lax.all_gather(w_qkv, "seq", axis=1, tiled=True),
+        jnp.concatenate(
+            lax.all_to_all(jnp.stack([w_qkv] * lax.axis_size("seq")), "seq", 0, 0), axis=1
+        ),
         preferred_element_type=jnp.float32,
     ).astype(jnp.bfloat16)
     block_len = min(128, tok_rows)

time: 535 us -> 750 us (1.40)
  the two profiles are of different devices: /device:TPU:2 before, /device:TPU:32 now
where the time goes in v1:
time: 750 us; the launch traced here: 749 us
  waiting for transfers between devices  475 us (63%)
  starting transfers between devices  121 us (16%)
  other arithmetic  92.7 us (12%)
  matrix products  27.9 us (4%)
  local copies, waits for them, and re-layouts  16.4 us (2%)
  between operations  13.6 us (2%)
    all_to_all x1, waiting for transfers between devices, per_device(): lax.all_to_all(jnp.stack([w_qkv] * lax.axis_size('seq')), 'seq', 0, 0)  289 us
    reduce_scatter x1, waiting for transfers between devices, per_device(): lax.psum_scatter(terms.astype(jnp.bfloat16), 'head', scatter_dimension=1,...  106 us
    ppermute x31, starting transfers between devices, passed_along(): lax.ppermute(value, axis, [(source, source + steps) for source in range(f...  106 us
    ppermute x31, waiting for transfers between devices, passed_along(): lax.ppermute(value, axis, [(source, source + steps) for source in range(f...  79.8 us
    another operation x10, other arithmetic, block_terms(): jax.scipy.linalg.solve_triangular(system, right_side, lower=True, unit_di...  78.9 us
    all_to_all x1, starting transfers between devices, per_device(): lax.all_to_all(jnp.stack([w_qkv] * lax.axis_size('seq')), 'seq', 0, 0)  15.5 us
  transfers between devices with their start and end apart: 34, of which 33 were waited for; matrix products, arithmetic and copies ran while one was open for 17% of the time, Pallas kernels for 0%

profile of v1, /device:TPU:32, one launch (start us, length us, event | category | flops | bytes accessed | tf_op | source)
XLA Modules:
  0.0 749.1 jit_solution(806952055239590490)
XLA Ops:
  7.8 4.2 stack.2
  12.0 15.5 %all-to-all-start = ((bf16[32,3,128,256]{2,3,1,0:T(8,128)(2,1)}), bf16[32,3,128,256]{2,3,1,0:T(8,128)(2,1)}, u32[]{:S(2)}, u32[]{:S(2)}) async-start(bf16[32,3,128,256]{2,3,1,0:T(8,128)(2,1)} %stack.2), calls=%async_computation | async-start | bytes 12582912 | tf_op jit(solution)/shard_map/all_to_all | solution.py:68
  29.4 288.8 %all-to-all-done = bf16[32,3,128,256]{2,3,1,0:T(8,128)(2,1)} async-done(((bf16[32,3,128,256]{2,3,1,0:T(8,128)(2,1)}), bf16[32,3,128,256]{2,3,1,0:T(8,128)(2,1)}, u32[]{:S(2)}, u32[]{:S(2)}) %all-to-all-start) | async-done | bytes 6291488 | tf_op jit(solution)/shard_map/all_to_all | solution.py:68
  318.1 4.6 fusion.81
  329.8 51.5 %while.37 = (s32[]{:T(128)}, f32[2,128,128]{2,1,0:T(8,128)S(1)}, f32[2,128,128]{2,1,0:T(8,128)S(1)}, s32[2,128]{1,0:T(2,128)}, f32[2,2,128,128]{3,2,1,0:T(8,128)...) while((s32[]{:T(128)}, f32[2,128,128]{2,1,0:T(8,128)S(1)}, ...), condition=%wide.region_4.6_spmd.clone, body=%wide.region_3.5_spmd.clone.sunk | while | flops 352977536 | bytes 3876507 | solution.py:107
  331.3 19.7 %custom-call.12 = f32[2,1,128,128]{2,3,1,0:T(8,128)S(1)} custom-call(f32[2,1,128,128]{3,2,1,0:T(8,128)S(1)} %fusion.175), custom_call_target="InvertDiagBlocksLowerTriangular" | custom-call | tf_op jit(solution)/shard_map/while/body/eval_jaxpr/jit(_solve_triangular)/vmap()/triangular_solve | solution.py:41
  357.0 19.7 %custom-call.12 = f32[2,1,128,128]{2,3,1,0:T(8,128)S(1)} custom-call(f32[2,1,128,128]{3,2,1,0:T(8,128)S(1)} %fusion.175), custom_call_target="InvertDiagBlocksLowerTriangular" | custom-call | tf_op jit(solution)/shard_map/while/body/eval_jaxpr/jit(_solve_triangular)/vmap()/triangular_solve | solution.py:41
  381.3 195.4 %while.38 = (s32[]{:T(128)}, f32[2,128,128]{2,1,0:T(8,128)S(1)}, f32[2,128,128]{2,1,0:T(8,128)S(1)}, f32[2,128,128]{2,1,0:T(8,128)S(1)}, s32[]{:T(128)}, /*index=5*/s32[]{:T(128)}) while((s32[]{:T(128)}, f32[2,128,128]{2,1,0:T(8,128)S(1)}, f32[2,128,128]{2,1,0:T(8,128)S(1)}, f32[2,128,128]{2,1,0:T(8,128)S(1)}, s32[]{:T(128)}, ...), condition=%wide.region_6.8_spmd.clone, body=%wide.region_5.7_spmd.clone.sunk | while | flops 50462720 | bytes 917623 | solution.py:116
  493.6 4.0 collective-permute-start
  499.5 5.2 collective-permute-start
  506.0 5.9 collective-permute-start
  513.1 5.9 collective-permute-start
  520.2 5.9 collective-permute-start
  527.3 5.9 collective-permute-start
  534.4 5.9 collective-permute-start
  541.5 5.9 collective-permute-start
  548.6 5.9 collective-permute-start
  555.7 5.9 collective-permute-start
  562.8 5.9 collective-permute-start
  569.9 5.9 collective-permute-start
  576.7 53.2 %while.36 = (s32[]{:T(128)}, f32[2,128,128]{2,1,0:T(8,128)S(1)}, f32[2,2,128,128]{3,2,1,0:T(8,128)}, s32[2,128]{1,0:T(2,128)}, f32[2,2,128,128]{3,2,1,0:T(8,128)...) while((s32[]{:T(128)}, f32[2,128,128]{2,1,0:T(8,128)S(1)}, ...), condition=%wide.region_9.11_spmd, body=%wide.region_8.10_spmd.sunk | while | flops 504103552 | bytes 7187665 | solution.py:123
  578.0 19.7 %custom-call.11 = f32[2,1,128,128]{2,3,1,0:T(8,128)S(1)} custom-call(f32[2,1,128,128]{3,2,1,0:T(8,128)S(1)} %fusion.160), custom_call_target="InvertDiagBlocksLowerTriangular" | custom-call | tf_op jit(solution)/shard_map/while/body/eval_jaxpr/jit(_solve_triangular)/vmap()/triangular_solve | solution.py:41
  604.6 19.7 %custom-call.11 = f32[2,1,128,128]{2,3,1,0:T(8,128)S(1)} custom-call(f32[2,1,128,128]{3,2,1,0:T(8,128)S(1)} %fusion.160), custom_call_target="InvertDiagBlocksLowerTriangular" | custom-call | tf_op jit(solution)/shard_map/while/body/eval_jaxpr/jit(_solve_triangular)/vmap()/triangular_solve | solution.py:41
  636.4 105.9 %reduce-scatter.2.cloned.1.call-done = bf16[256,256]{1,0:T(8,128)(2,1)} async-done(((bf16[256,4096]{1,0:T(8,128)(2,1)}), bf16[256,256]{1,0:T(8,128)(2,1)}) %reduce-scatter.2.cloned.1.call-update) | async-done | bytes 131088 | tf_op jit(solution)/shard_map/reduce_scatter | solution.py:130
  (239 shorter events, 167.6 us)
Async XLA Ops:
  12.0 306.2 %all-to-all-start = ((bf16[32,3,128,256]{2,3,1,0:T(8,128)(2,1)}), bf16[32,3,128,256]{2,3,1,0:T(8,128)(2,1)}, u32[]{:S(2)}, u32[]{:S(2)}) async-start(bf16[32,3,128,256]{2,3,1,0:T(8,128)(2,1)} %stack.2), calls=%async_computation | async-start | bytes 12582912 | tf_op jit(solution)/shard_map/all_to_all | solution.py:68
  27.5 604.9 %all-gather.2.cloned.1.call-start = ((), (), s32[]{:S(2)}) async-start(), calls=%async_computation.2 | async-start | bytes 2162688 | tf_op jit(solution)/shard_map/all_gather | solution.py:128
  28.3 714.0 %reduce-scatter.2.cloned.1.call-start = ((), (), s32[]{:S(2)}) async-start(), calls=%async_computation.3 | async-start | bytes 2228224 | tf_op jit(solution)/shard_map/reduce_scatter | solution.py:130
  381.6 5.6 collective-permute-start
  387.5 5.6 collective-permute-start
  393.4 5.6 collective-permute-start
  399.3 5.6 collective-permute-start
  405.2 5.6 collective-permute-start
  411.1 5.6 collective-permute-start
  417.0 5.6 collective-permute-start
  422.9 5.6 collective-permute-start
  428.8 5.6 collective-permute-start
  434.7 5.6 collective-permute-start
  499.5 6.1 collective-permute-start
  506.0 6.8 collective-permute-start
  513.1 6.8 collective-permute-start
  520.2 6.8 collective-permute-start
  527.3 6.8 collective-permute-start
  534.4 6.8 collective-permute-start
  541.5 6.8 collective-permute-start
  548.6 6.8 collective-permute-start
  555.7 6.8 collective-permute-start
  562.8 6.8 collective-permute-start
  569.9 6.8 collective-permute-start
  (18 other events, 607.3 us)
Sparse Core Ops, SparseCore 0:
  30.4 152.9 all-gather.1
  636.5 105.6 reduce-scatter.1
